TPU v7x, 128 devices: a whole 4x4x4 slice. The times are simulated.
128 devices in a mesh: dp: 8 (over x, core), ctx: 16 (over z, y).
Axes of the slice: x: 4, y: 4, z: 4, core: 2. Of those that a mesh axis runs over, the one named last changes fastest.
Arguments:
- queries: bfloat16 [8, 2048, 2048], P('dp', 'ctx'), may hold values from -6 to 6
- keys: bfloat16 [8, 2048, 2048], P('dp', 'ctx'), may hold values from -6 to 6
- values: bfloat16 [8, 2048, 2048], P('dp', 'ctx'), may hold values from -6 to 6
- cotangent: bfloat16 [8, 2048, 2048], P('dp', 'ctx'), may hold values from -6 to 6
- doc_lengths: int32 [8, 4], P('dp'), may hold values from 0 to 2048, as said below
- filter_taps: float32 [2048, 2048], P('ctx'), may hold values from -0.13258252 to 0.13258252
Outputs:
- hyena_out: bfloat16 [8, 2048, 2048], P('dp', 'ctx')
- grad_queries: bfloat16 [8, 2048, 2048], P('dp', 'ctx')
- grad_keys: bfloat16 [8, 2048, 2048], P('dp', 'ctx')
- grad_values: bfloat16 [8, 2048, 2048], P('dp', 'ctx')
- grad_filter: float32 [2048, 2048], P('ctx', 'dp')
Inputs may be any that keep to these rules, and one draw needn't show every extreme that they name: `doc_lengths`: each row holds 4 document lengths that sum to 2048; a length may be zero (an unused slot); in every draw some row holds a single document of all 2048 positions.
All inputs are finite; a program needn't handle non-finite values.
Results may differ from a plain program's by a relative error of at most 0.0051.
Values may be sent and summed in bfloat16 or wider, within the bound.
No kernel may reach another device: no remote copies, remote signals or barrier semaphores. Data moves between devices by JAX's collectives and lax.ppermute only.
A program may use at most 512 MiB of HBM per device.

v0:
```python
import functools

import jax
import jax.numpy as jnp
from jax import lax
from jax.experimental import pallas as pl
from jax.experimental.pallas import tpu as pltpu
from jax.sharding import PartitionSpec as P

BLOCK = 128
SEQS = 8
BLOCKS = 16
PEERS = SEQS * BLOCKS
OWN = 16
DOCS = 4
ROWS = 40
FILT, DOC = 2 * OWN, 2 * OWN + 2
F32, BF16 = jnp.float32, jnp.bfloat16


def iota(axis, shape=(BLOCK, BLOCK)):
    return lax.broadcasted_iota(jnp.int32, shape, axis)


def dot(a, b):
    return jnp.dot(a, b, preferred_element_type=F32)


def dot_nt(a, b):
    return lax.dot_general(a, b, (((1,), (1,)), ((), ())), preferred_element_type=F32)


def eye_rev():
    row, col = iota(0), iota(1)
    return (row == col).astype(F32).astype(BF16), (row + col == BLOCK - 1).astype(F32).astype(BF16)


def put(ref, start, stride, tile):
    for r in range(tile.shape[0] // 8):
        ref[pl.ds(start + r * 8 * stride, 8, stride=stride), :] = tile[8 * r : 8 * r + 8]


def take(ref, start, stride, rows):
    return jnp.concatenate(
        [ref[pl.ds(start + r * 8 * stride, 8, stride=stride), :] for r in range(rows // 8)], axis=0
    )


def pack_kernel(len_ref, q_ref, k_ref, v_ref, c_ref, filt_hbm, out_ref, stage, filt, sem):
    step = pl.program_id(0)
    tiles = q_ref.shape[2] // BLOCK
    eye, rev = eye_rev()
    copy = pltpu.make_async_copy(
        filt_hbm.at[:, pl.ds(pl.multiple_of(lax.axis_index("dp") * 2 * BLOCK, BLOCK), 2 * BLOCK)],
        filt,
        sem,
    )

    @pl.when(step == 0)
    def _():
        copy.start()
        lane = iota(1, (8, BLOCK))
        pos = lax.axis_index("ctx") * BLOCK + lane
        pos_rev = lax.axis_index("ctx") * BLOCK + BLOCK - 1 - lane
        doc = jnp.zeros((8, BLOCK), F32)
        doc_rev = jnp.zeros((8, BLOCK), F32)
        end = jnp.int32(0)
        for i in range(DOCS):
            end = end + len_ref[0, i]
            doc = doc + (end <= pos).astype(F32)
            doc_rev = doc_rev + (end <= pos_rev).astype(F32)
        zero = jnp.zeros((8, BLOCK), F32)
        for r in range(PEERS // 8):
            put(stage, DOC + r * 8 * ROWS, ROWS, doc)
            put(stage, DOC + 1 + r * 8 * ROWS, ROWS, doc_rev)
            for extra in range(DOC + 2, ROWS):
                put(stage, extra + r * 8 * ROWS, ROWS, zero)

    for i in range(tiles):
        tile = step * tiles + i
        lanes = pl.ds(i * BLOCK, BLOCK)
        gated = (k_ref[0, :, lanes].astype(F32) * v_ref[0, :, lanes].astype(F32)).astype(BF16)
        weighted = (c_ref[0, :, lanes].astype(F32) * q_ref[0, :, lanes].astype(F32)).astype(BF16)
        put(stage, tile, ROWS, dot_nt(eye, gated))
        put(stage, OWN + tile, ROWS, dot_nt(eye, dot(rev, weighted).astype(BF16)))

    @pl.when(step == pl.num_programs(0) - 1)
    def _():
        copy.wait()
        for i in range(2):
            put(stage, FILT + i, ROWS, dot_nt(eye, filt[:, i * BLOCK : (i + 1) * BLOCK].astype(BF16)))
        out_ref[...] = stage[...].reshape(PEERS, ROWS, BLOCK).astype(BF16)


def conv_kernel(in_ref, out_ref, src, dst, mask, rel, rel_t, keep, stack, extra, taps, cross):
    row, col = iota(0), iota(1)
    far = ROWS * BLOCKS
    src[...] = in_ref[...].astype(F32).reshape(PEERS * ROWS, BLOCK)
    dst[...] = jnp.zeros_like(dst)
    stack[...] = jnp.zeros_like(stack)
    cross[:, BLOCKS * BLOCK :] = jnp.zeros((BLOCK, BLOCK), F32)

    def blocks(line, backward=False):
        order = range(BLOCKS - 1, -1, -1) if backward else range(BLOCKS)
        return jnp.concatenate([src[pl.ds(b * ROWS + line, 8, stride=far), :] for b in order], axis=0)

    for way, doc in enumerate((blocks(DOC), blocks(DOC + 1, True))):
        head = jnp.broadcast_to(doc[:, :1], (BLOCK, BLOCK))
        for d in range(BLOCKS):
            same = (doc[: BLOCK - 8 * d] == head[8 * d :]).astype(F32)
            if d:
                same = jnp.concatenate([jnp.zeros((8 * d, BLOCK), F32), same], axis=0)
            mask[way * BLOCK : (way + 1) * BLOCK, d * BLOCK : (d + 1) * BLOCK] = same.astype(BF16)
        for k in range(DOCS):
            at = (jnp.abs(doc - head) == k).astype(F32)
            keep[k, way * BLOCK : (way + 1) * BLOCK, :] = at
            rel[k, way * BLOCK : (way + 1) * BLOCK, :] = at.astype(BF16)
    doc, flipped = blocks(DOC), blocks(DOC + 1)
    head = jnp.broadcast_to(doc[:, :1], (BLOCK, BLOCK))
    for k in range(DOCS):
        rel_t[k] = jnp.transpose((flipped - head == k).astype(F32)).astype(BF16)

    def channel(t, carry):
        wn = blocks(OWN + t)
        for way, signal in enumerate((blocks(t), blocks(OWN + t, True))):
            even = signal.astype(BF16)
            odd = jnp.concatenate([jnp.zeros((8, BLOCK), F32), signal[: BLOCK - 8]], axis=0).astype(BF16)
            for d in range(BLOCKS):
                down = d // 2 * 16
                at = (slice(way * BLOCK + down, (way + 1) * BLOCK), slice(d * BLOCK, (d + 1) * BLOCK))
                stack[at] = (odd if d % 2 else even)[: BLOCK - down] * mask[at]
            for k in range(1, DOCS):
                extra[k, way * BLOCK : (way + 1) * BLOCK, :] = even * rel[k, way * BLOCK : (way + 1) * BLOCK, :]
        line = (t // 2) * far + FILT + t % 2
        before = jnp.zeros((BLOCK, BLOCK), F32)
        for d in range(BLOCKS):
            lags = jnp.broadcast_to(src[pl.ds(line + d * ROWS, 1), :], (BLOCK, BLOCK))
            turned = pltpu.roll(lags, 0, 1, stride=1, stride_axis=0)
            taps[d * BLOCK : (d + 1) * BLOCK, :] = jnp.where(col >= row, turned, before).astype(BF16)
            before = turned
        out = keep[0] * dot(stack[...], taps[...])
        for k in range(1, DOCS):
            out = out + keep[k] * dot(extra[k], taps[:BLOCK])
        for b in range(BLOCKS):
            dst[pl.ds(b * ROWS + t, 8, stride=far), :] = out[8 * b : 8 * b + 8]
            dst[pl.ds((BLOCKS - 1 - b) * ROWS + OWN + t, 8, stride=far), :] = out[BLOCK + 8 * b : BLOCK + 8 * b + 8]
        wt = jnp.transpose(wn).astype(BF16)
        cross[:, : BLOCKS * BLOCK] = dot(wt * rel_t[0], stack[:BLOCK, :])
        for k in range(1, DOCS):
            cross[:, :BLOCK] += dot(wt * rel_t[k], extra[k, :BLOCK, :])
        sums = []
        for d in range(BLOCKS):
            here = cross[:, d * BLOCK : (d + 1) * BLOCK]
            there = cross[:, (d + 1) * BLOCK : (d + 2) * BLOCK]
            lined = jnp.where(row + col <= BLOCK - 1, here, there)
            sums.append(jnp.sum(pltpu.roll(lined, 1, 1, stride=1, stride_axis=0), axis=0, keepdims=True))
        grad = jnp.concatenate(sums, axis=0)
        high = grad.astype(BF16).astype(F32)
        put(dst, line, ROWS, high)
        put(dst, line + 2, ROWS, grad - high)
        return carry

    lax.fori_loop(0, OWN, channel, 0)
    out_ref[...] = dst[...].reshape(PEERS, ROWS, BLOCK).astype(BF16)


def finish_kernel(q_ref, k_ref, v_ref, c_ref, in_ref, ho_ref, gq_ref, gk_ref, gv_ref, gf_ref, stage):
    step = pl.program_id(0)
    tiles = q_ref.shape[2] // BLOCK
    eye, rev = eye_rev()

    @pl.when(step == 0)
    def _():
        stage[...] = in_ref[...].astype(F32).reshape(PEERS * ROWS, BLOCK)
        turn = ((iota(0) + iota(1)) % BLOCK == 0).astype(F32).astype(BF16)
        for i in range(2):
            high = take(stage, FILT + i, ROWS, PEERS).astype(BF16)
            low = take(stage, FILT + 2 + i, ROWS, PEERS).astype(BF16)
            gf_ref[:, i * BLOCK : (i + 1) * BLOCK] = dot_nt(turn, high) + dot_nt(turn, low)

    for i in range(tiles):
        tile = step * tiles + i
        lanes = pl.ds(i * BLOCK, BLOCK)
        conv = dot_nt(eye, take(stage, tile, ROWS, PEERS).astype(BF16))
        grad = dot_nt(rev, take(stage, OWN + tile, ROWS, PEERS).astype(BF16))
        ho_ref[0, :, lanes] = (q_ref[0, :, lanes].astype(F32) * conv).astype(BF16)
        gq_ref[0, :, lanes] = (c_ref[0, :, lanes].astype(F32) * conv).astype(BF16)
        gk_ref[0, :, lanes] = (grad * v_ref[0, :, lanes].astype(F32)).astype(BF16)
        gv_ref[0, :, lanes] = (grad * k_ref[0, :, lanes].astype(F32)).astype(BF16)


def body(queries, keys, values, cotangent, doc_lengths, filter_taps):
    width = 512
    steps = queries.shape[2] // width
    tile = pl.BlockSpec((1, BLOCK, width), lambda i: (0, 0, i))
    whole = pl.BlockSpec((PEERS, ROWS, BLOCK), lambda i: (0, 0, 0))
    message = jax.ShapeDtypeStruct((PEERS, ROWS, BLOCK), BF16)
    params = pltpu.CompilerParams(vmem_limit_bytes=32 << 20)
    packed = pl.pallas_call(
        pack_kernel,
        grid=(steps,),
        in_specs=[pl.BlockSpec(memory_space=pltpu.SMEM), tile, tile, tile, tile, pl.BlockSpec(memory_space=pl.ANY)],
        out_specs=whole,
        out_shape=message,
        scratch_shapes=[
            pltpu.VMEM((PEERS * ROWS, BLOCK), F32),
            pltpu.VMEM((BLOCK, 2 * BLOCK), F32),
            pltpu.SemaphoreType.DMA,
        ],
        compiler_params=params,
        name="pack",
    )(doc_lengths, queries, keys, values, cotangent, filter_taps)
    arrived = lax.all_to_all(packed, ("dp", "ctx"), 0, 0, tiled=True)
    results = pl.pallas_call(
        conv_kernel,
        in_specs=[pl.BlockSpec(memory_space=pltpu.VMEM)],
        out_specs=pl.BlockSpec(memory_space=pltpu.VMEM),
        out_shape=message,
        scratch_shapes=[
            pltpu.VMEM((PEERS * ROWS, BLOCK), F32),
            pltpu.VMEM((PEERS * ROWS, BLOCK), F32),
            pltpu.VMEM((2 * BLOCK, BLOCKS * BLOCK), BF16),
            pltpu.VMEM((DOCS, 2 * BLOCK, BLOCK), BF16),
            pltpu.VMEM((DOCS, BLOCK, BLOCK), BF16),
            pltpu.VMEM((DOCS, 2 * BLOCK, BLOCK), F32),
            pltpu.VMEM((2 * BLOCK, BLOCKS * BLOCK), BF16),
            pltpu.VMEM((DOCS, 2 * BLOCK, BLOCK), BF16),
            pltpu.VMEM((BLOCKS * BLOCK, BLOCK), BF16),
            pltpu.VMEM((BLOCK, (BLOCKS + 1) * BLOCK), F32),
        ],
        compiler_params=params,
        name="conv",
    )(arrived)
    returned = lax.all_to_all(results, ("dp", "ctx"), 0, 0, tiled=True)
    row_out = jax.ShapeDtypeStruct(queries.shape, BF16)
    return pl.pallas_call(
        finish_kernel,
        grid=(steps,),
        in_specs=[tile, tile, tile, tile, whole],
        out_specs=[tile, tile, tile, tile, pl.BlockSpec((BLOCK, 2 * BLOCK), lambda i: (0, 0))],
        out_shape=[row_out, row_out, row_out, row_out, jax.ShapeDtypeStruct((BLOCK, 2 * BLOCK), F32)],
        scratch_shapes=[pltpu.VMEM((PEERS * ROWS, BLOCK), F32)],
        compiler_params=params,
        name="finish",
    )(queries, keys, values, cotangent, returned)


def solution(mesh):
    rows = P("dp", "ctx", None)
    return jax.shard_map(
        body,
        mesh=mesh,
        in_specs=(rows, rows, rows, rows, P("dp", None), P("ctx", None)),
        out_specs=(rows, rows, rows, rows, P("ctx", "dp")),
        check_vma=False,
    )
```

profile of v0, /device:TPU:0, one launch (start us, length us, event | category | flops | bytes accessed | tf_op | source)
XLA Modules:
  0.0 91.1 jit_solution(799528589905520180)
XLA Ops:
  0.6 0.0 copy-start
  0.6 1.0 %copy-done = bf16[1,128,2048]{2,1,0:T(8,128)(2,1)S(1)} copy-done((bf16[1,128,2048]{2,1,0:T(8,128)(2,1)S(1)}, bf16[1,128,2048]{2,1,0:T(8,128)(2,1)}, u32[]{:S(2)}) %copy-start) | copy-done | bytes 524312
  1.7 0.0 copy-start.2
  1.7 1.0 %copy-done.2 = bf16[1,128,2048]{2,1,0:T(8,128)(2,1)S(1)} copy-done((bf16[1,128,2048]{2,1,0:T(8,128)(2,1)S(1)}, bf16[1,128,2048]{2,1,0:T(8,128)(2,1)}, u32[]{:S(2)}) %copy-start.2) | copy-done | bytes 524312
  2.7 0.0 copy-start.4
  2.7 1.0 %copy-done.4 = bf16[1,128,2048]{2,1,0:T(8,128)(2,1)S(1)} copy-done((bf16[1,128,2048]{2,1,0:T(8,128)(2,1)S(1)}, bf16[1,128,2048]{2,1,0:T(8,128)(2,1)}, u32[]{:S(2)}) %copy-start.4) | copy-done | bytes 524312
  3.8 0.0 copy-start.6
  3.8 1.0 %copy-done.6 = bf16[1,128,2048]{2,1,0:T(8,128)(2,1)S(1)} copy-done((bf16[1,128,2048]{2,1,0:T(8,128)(2,1)S(1)}, bf16[1,128,2048]{2,1,0:T(8,128)(2,1)}, u32[]{:S(2)}) %copy-start.6) | copy-done | bytes 524312
  4.8 0.0 copy-start.8
  4.8 1.2 %copy-done.8 = f32[128,2048]{1,0:T(8,128)S(1)} copy-done((f32[128,2048]{1,0:T(8,128)S(1)}, f32[128,2048]{1,0:T(8,128)}, u32[]{:S(2)}) %copy-start.8) | copy-done | bytes 1048600
  6.0 0.7 copy-done.9
  6.7 4.0 %pack.1 = bf16[128,40,128]{2,1,0:T(8,128)(2,1)S(1)} custom-call(s32[1,4]{1,0:T(1,128)S(1)} %copy-done.9, bf16[1,128,2048]{2,1,0:T(8,128)(2,1)S(1)} %copy-done, bf16[1,128,2048]{2,1,0:T(8,128)(2,1)S(1)} %copy-done.2, bf16[1,128,2048]{2,1,0:T(8,128)(2,1)S(1)} %copy-done.4, bf16[1,128,2048]{2,1,0:T(8,128)(2,1)S(1)} %copy-done.6, f32[128,2048]{1,0:T(8,128)S(1)} %copy-done.8), custom_call_target="tpu_custom_call" | custom-call | tf_op jit(solution)/shard_map/pack/pallas_call | solution.py:199
  10.7 32.7 %all_to_all.10.in_ref = bf16[128,40,128]{2,1,0:T(8,128)(2,1)S(1)} all-to-all(bf16[128,40,128]{2,1,0:T(8,128)(2,1)S(1)} %pack.1), channel_id=1, replica_groups=mesh['dp'=8,'ctx'=16] {'dp','ctx'}, dimensions={0} | all-to-all | bytes 2621440 | tf_op jit(solution)/shard_map/all_to_all | solution.py:213
  43.4 18.6 %conv.1 = bf16[128,40,128]{2,1,0:T(8,128)(2,1)S(1)} custom-call(bf16[128,40,128]{2,1,0:T(8,128)(2,1)S(1)} %all_to_all.10.in_ref), custom_call_target="tpu_custom_call" | custom-call | tf_op jit(solution)/shard_map/conv/pallas_call | solution.py:214
  62.0 0.0 copy-start.1
  62.0 0.0 copy-start.3
  62.0 0.0 copy-start.5
  62.0 0.0 copy-start.7
  62.1 25.9 %all_to_all.11.in_ref = bf16[128,40,128]{2,1,0:T(8,128)(2,1)S(1)} all-to-all(bf16[128,40,128]{2,1,0:T(8,128)(2,1)S(1)} %conv.1), channel_id=1, replica_groups=mesh['dp'=8,'ctx'=16] {'dp','ctx'}, dimensions={0} | all-to-all | bytes 2621440 | tf_op jit(solution)/shard_map/all_to_all | solution.py:234
  87.9 0.0 copy-done.1
  87.9 0.0 copy-done.3
  87.9 0.0 copy-done.5
  88.0 0.0 copy-done.7
  88.0 3.2 %finish.1 = (bf16[1,128,2048]{2,1,0:T(8,128)(2,1)}, bf16[1,128,2048]{2,1,0:T(8,128)(2,1)}, bf16[1,128,2048]{2,1,0:T(8,128)(2,1)}, bf16[1,128,2048]{2,1,0:T(8,128)(2,1)}, f32[128,256]{1,0:T(8,128)}) custom-call(bf16[1,128,2048]{2,1,0:T(8,128)(2,1)S(1)} %copy-done.1, bf16[1,128,2048]{2,1,0:T(8,128)(2,1)S(1)} %copy-done.3, bf16[1,128,2048]{2,1,0:T(8,128)(2,1)S(1)} %copy-done.5, ...), custom_call_target="tpu_custom_call" | custom-call | tf_op jit(solution)/shard_map/finish/pallas_call | solution.py:236
  (1 shorter events, 0.0 us)
Async XLA Ops:
  0.6 1.0 %copy-start = (bf16[1,128,2048]{2,1,0:T(8,128)(2,1)S(1)}, bf16[1,128,2048]{2,1,0:T(8,128)(2,1)}, u32[]{:S(2)}) copy-start(bf16[1,128,2048]{2,1,0:T(8,128)(2,1)} %q_ref.3) | copy-start | bytes 1572868
  1.7 1.0 %copy-start.2 = (bf16[1,128,2048]{2,1,0:T(8,128)(2,1)S(1)}, bf16[1,128,2048]{2,1,0:T(8,128)(2,1)}, u32[]{:S(2)}) copy-start(bf16[1,128,2048]{2,1,0:T(8,128)(2,1)} %k_ref.3) | copy-start | bytes 1572868
  2.7 1.0 %copy-start.4 = (bf16[1,128,2048]{2,1,0:T(8,128)(2,1)S(1)}, bf16[1,128,2048]{2,1,0:T(8,128)(2,1)}, u32[]{:S(2)}) copy-start(bf16[1,128,2048]{2,1,0:T(8,128)(2,1)} %v_ref.3) | copy-start | bytes 1572868
  3.8 1.0 %copy-start.6 = (bf16[1,128,2048]{2,1,0:T(8,128)(2,1)S(1)}, bf16[1,128,2048]{2,1,0:T(8,128)(2,1)}, u32[]{:S(2)}) copy-start(bf16[1,128,2048]{2,1,0:T(8,128)(2,1)} %c_ref.3) | copy-start | bytes 1572868
  4.8 1.2 %copy-start.8 = (f32[128,2048]{1,0:T(8,128)S(1)}, f32[128,2048]{1,0:T(8,128)}, u32[]{:S(2)}) copy-start(f32[128,2048]{1,0:T(8,128)} %filt_hbm.1) | copy-start | bytes 3145732
  6.0 0.7 copy-start.9
  62.0 25.9 %copy-start.1 = (bf16[1,128,2048]{2,1,0:T(8,128)(2,1)S(1)}, bf16[1,128,2048]{2,1,0:T(8,128)(2,1)}, u32[]{:S(2)}) copy-start(bf16[1,128,2048]{2,1,0:T(8,128)(2,1)} %q_ref.3) | copy-start | bytes 1572868
  62.0 25.9 %copy-start.3 = (bf16[1,128,2048]{2,1,0:T(8,128)(2,1)S(1)}, bf16[1,128,2048]{2,1,0:T(8,128)(2,1)}, u32[]{:S(2)}) copy-start(bf16[1,128,2048]{2,1,0:T(8,128)(2,1)} %k_ref.3) | copy-start | bytes 1572868
  62.0 25.9 %copy-start.5 = (bf16[1,128,2048]{2,1,0:T(8,128)(2,1)S(1)}, bf16[1,128,2048]{2,1,0:T(8,128)(2,1)}, u32[]{:S(2)}) copy-start(bf16[1,128,2048]{2,1,0:T(8,128)(2,1)} %v_ref.3) | copy-start | bytes 1572868
  62.0 25.9 %copy-start.7 = (bf16[1,128,2048]{2,1,0:T(8,128)(2,1)S(1)}, bf16[1,128,2048]{2,1,0:T(8,128)(2,1)}, u32[]{:S(2)}) copy-start(bf16[1,128,2048]{2,1,0:T(8,128)(2,1)} %c_ref.3) | copy-start | bytes 1572868
where the time goes:
time: 91.5 us; the launch traced here: 91.1 us
  blocking collectives  58.6 us (64%)
  Pallas kernels  25.8 us (28%)
  local copies, waits for them, and re-layouts  6.06 us (7%)
    all_to_all x1, blocking collectives, body(): arrived = lax.all_to_all(packed, ('dp', 'ctx'), 0, 0, tiled=True)  32.7 us
    all_to_all x1, blocking collectives, body(): returned = lax.all_to_all(results, ('dp', 'ctx'), 0, 0, tiled=True)  25.9 us
    pallas_call x1, Pallas kernels, body(): pl.pallas_call(conv_kernel, in_specs=[pl.BlockSpec(memory_space=pltpu.VME...  18.6 us
    unnamed x20, local copies, waits for them, and re-layouts  6.06 us
    pallas_call x1, Pallas kernels, body(): pl.pallas_call(pack_kernel, grid=(steps,), in_specs=[pl.BlockSpec(memory_...  3.97 us
    pallas_call x1, Pallas kernels, body(): pl.pallas_call(finish_kernel, grid=(steps,), in_specs=[tile, tile, tile,...  3.18 us

commit v1 on v0

--- a/solution.py
+++ b/solution.py
@@ -28,6 +28,10 @@
 
 def dot_nt(a, b):
     return lax.dot_general(a, b, (((1,), (1,)), ((), ())), preferred_element_type=F32)
+
+
+def dot_tn(a, b):
+    return lax.dot_general(a, b, (((0,), (0,)), ((), ())), preferred_element_type=F32)
 
 
 def eye_rev():
@@ -76,29 +80,29 @@
             for extra in range(DOC + 2, ROWS):
                 put(stage, extra + r * 8 * ROWS, ROWS, zero)
 
+    gated = dot_tn((k_ref[0].astype(F32) * v_ref[0].astype(F32)).astype(BF16), eye)
+    weighted = dot_tn((c_ref[0].astype(F32) * q_ref[0].astype(F32)).astype(BF16), rev)
     for i in range(tiles):
-        tile = step * tiles + i
-        lanes = pl.ds(i * BLOCK, BLOCK)
-        gated = (k_ref[0, :, lanes].astype(F32) * v_ref[0, :, lanes].astype(F32)).astype(BF16)
-        weighted = (c_ref[0, :, lanes].astype(F32) * q_ref[0, :, lanes].astype(F32)).astype(BF16)
-        put(stage, tile, ROWS, dot_nt(eye, gated))
-        put(stage, OWN + tile, ROWS, dot_nt(eye, dot(rev, weighted).astype(BF16)))
+        part = slice(i * BLOCK, (i + 1) * BLOCK)
+        put(stage, step * tiles + i, ROWS, gated[part])
+        put(stage, OWN + step * tiles + i, ROWS, weighted[part])
 
     @pl.when(step == pl.num_programs(0) - 1)
     def _():
         copy.wait()
+        lags = dot_tn(filt[...].astype(BF16), eye)
         for i in range(2):
-            put(stage, FILT + i, ROWS, dot_nt(eye, filt[:, i * BLOCK : (i + 1) * BLOCK].astype(BF16)))
+            put(stage, FILT + i, ROWS, lags[i * BLOCK : (i + 1) * BLOCK])
         out_ref[...] = stage[...].reshape(PEERS, ROWS, BLOCK).astype(BF16)
 
 
-def conv_kernel(in_ref, out_ref, src, dst, mask, rel, rel_t, keep, stack, extra, taps, cross):
+def conv_kernel(in_ref, out_ref, src, dst, mask, rel, rel_t, keep, stack, extra, taps, cross, fold):
     row, col = iota(0), iota(1)
     far = ROWS * BLOCKS
     src[...] = in_ref[...].astype(F32).reshape(PEERS * ROWS, BLOCK)
     dst[...] = jnp.zeros_like(dst)
     stack[...] = jnp.zeros_like(stack)
-    cross[:, BLOCKS * BLOCK :] = jnp.zeros((BLOCK, BLOCK), F32)
+    cross[...] = jnp.zeros_like(cross)
 
     def blocks(line, backward=False):
         order = range(BLOCKS - 1, -1, -1) if backward else range(BLOCKS)
@@ -120,47 +124,68 @@
     for k in range(DOCS):
         rel_t[k] = jnp.transpose((flipped - head == k).astype(F32)).astype(BF16)
 
-    def channel(t, carry):
-        wn = blocks(OWN + t)
+    def build(t, slot):
         for way, signal in enumerate((blocks(t), blocks(OWN + t, True))):
             even = signal.astype(BF16)
             odd = jnp.concatenate([jnp.zeros((8, BLOCK), F32), signal[: BLOCK - 8]], axis=0).astype(BF16)
             for d in range(BLOCKS):
                 down = d // 2 * 16
                 at = (slice(way * BLOCK + down, (way + 1) * BLOCK), slice(d * BLOCK, (d + 1) * BLOCK))
-                stack[at] = (odd if d % 2 else even)[: BLOCK - down] * mask[at]
+                stack[(slot,) + at] = (odd if d % 2 else even)[: BLOCK - down] * mask[at]
             for k in range(1, DOCS):
-                extra[k, way * BLOCK : (way + 1) * BLOCK, :] = even * rel[k, way * BLOCK : (way + 1) * BLOCK, :]
+                extra[slot, k, way * BLOCK : (way + 1) * BLOCK, :] = even * rel[k, way * BLOCK : (way + 1) * BLOCK, :]
         line = (t // 2) * far + FILT + t % 2
-        before = jnp.zeros((BLOCK, BLOCK), F32)
+        before = jnp.zeros((BLOCK, BLOCK), BF16)
         for d in range(BLOCKS):
-            lags = jnp.broadcast_to(src[pl.ds(line + d * ROWS, 1), :], (BLOCK, BLOCK))
+            lags = jnp.broadcast_to(src[pl.ds(line + d * ROWS, 1), :], (BLOCK, BLOCK)).astype(BF16)
             turned = pltpu.roll(lags, 0, 1, stride=1, stride_axis=0)
-            taps[d * BLOCK : (d + 1) * BLOCK, :] = jnp.where(col >= row, turned, before).astype(BF16)
+            taps[slot, d * BLOCK : (d + 1) * BLOCK, :] = jnp.where(col >= row, turned, before)
             before = turned
-        out = keep[0] * dot(stack[...], taps[...])
+
+    def multiply(t, slot):
+        out = keep[0] * dot(stack[slot], taps[slot])
         for k in range(1, DOCS):
-            out = out + keep[k] * dot(extra[k], taps[:BLOCK])
+            out = out + keep[k] * dot(extra[slot, k], taps[slot, :BLOCK])
         for b in range(BLOCKS):
             dst[pl.ds(b * ROWS + t, 8, stride=far), :] = out[8 * b : 8 * b + 8]
             dst[pl.ds((BLOCKS - 1 - b) * ROWS + OWN + t, 8, stride=far), :] = out[BLOCK + 8 * b : BLOCK + 8 * b + 8]
-        wt = jnp.transpose(wn).astype(BF16)
-        cross[:, : BLOCKS * BLOCK] = dot(wt * rel_t[0], stack[:BLOCK, :])
+        wt = jnp.transpose(blocks(OWN + t)).astype(BF16)
+        cross[slot, :, : BLOCKS * BLOCK] = dot(wt * rel_t[0], stack[slot, :BLOCK, :])
         for k in range(1, DOCS):
-            cross[:, :BLOCK] += dot(wt * rel_t[k], extra[k, :BLOCK, :])
-        sums = []
+            cross[slot, :, :BLOCK] += dot(wt * rel_t[k], extra[slot, k, :BLOCK, :])
+
+    def gather(t, slot):
+        line = (t // 2) * far + FILT + t % 2
+        sums = [jnp.zeros((8, BLOCK), F32)] * BLOCKS
+        for k in range(BLOCK // 8):
+            part = slice(8 * k, 8 * k + 8)
+            lower = 8 * k + iota(0, (8, BLOCK)) + iota(1, (8, BLOCK)) <= BLOCK - 1
+            here = cross[slot, part, :BLOCK]
+            for d in range(BLOCKS):
+                there = cross[slot, part, (d + 1) * BLOCK : (d + 2) * BLOCK]
+                sums[d] += pltpu.roll(jnp.where(lower, here, there), 8 * k + 1, 1, stride=1, stride_axis=0)
+                here = there
         for d in range(BLOCKS):
-            here = cross[:, d * BLOCK : (d + 1) * BLOCK]
-            there = cross[:, (d + 1) * BLOCK : (d + 2) * BLOCK]
-            lined = jnp.where(row + col <= BLOCK - 1, here, there)
-            sums.append(jnp.sum(pltpu.roll(lined, 1, 1, stride=1, stride_axis=0), axis=0, keepdims=True))
-        grad = jnp.concatenate(sums, axis=0)
+            fold[slot, 8 * d : 8 * d + 8, :] = sums[d]
+        grad = sum(fold[slot, pl.ds(i, BLOCKS, stride=8), :] for i in range(8))
         high = grad.astype(BF16).astype(F32)
         put(dst, line, ROWS, high)
         put(dst, line + 2, ROWS, grad - high)
+
+    build(0, 0)
+
+    def pair(u, carry):
+        t = 2 * u
+        multiply(t, 0)
+        build(t + 1, 1)
+        gather(jnp.maximum(t - 1, 0), 1)
+        multiply(t + 1, 1)
+        build(jnp.minimum(t + 2, OWN - 1), 0)
+        gather(t, 0)
         return carry
 
-    lax.fori_loop(0, OWN, channel, 0)
+    lax.fori_loop(0, OWN // 2, pair, 0)
+    gather(OWN - 1, 1)
     out_ref[...] = dst[...].reshape(PEERS, ROWS, BLOCK).astype(BF16)
 
 
@@ -178,15 +203,17 @@
             low = take(stage, FILT + 2 + i, ROWS, PEERS).astype(BF16)
             gf_ref[:, i * BLOCK : (i + 1) * BLOCK] = dot_nt(turn, high) + dot_nt(turn, low)
 
-    for i in range(tiles):
-        tile = step * tiles + i
-        lanes = pl.ds(i * BLOCK, BLOCK)
-        conv = dot_nt(eye, take(stage, tile, ROWS, PEERS).astype(BF16))
-        grad = dot_nt(rev, take(stage, OWN + tile, ROWS, PEERS).astype(BF16))
-        ho_ref[0, :, lanes] = (q_ref[0, :, lanes].astype(F32) * conv).astype(BF16)
-        gq_ref[0, :, lanes] = (c_ref[0, :, lanes].astype(F32) * conv).astype(BF16)
-        gk_ref[0, :, lanes] = (grad * v_ref[0, :, lanes].astype(F32)).astype(BF16)
-        gv_ref[0, :, lanes] = (grad * k_ref[0, :, lanes].astype(F32)).astype(BF16)
+    def rows(first):
+        return jnp.concatenate(
+            [take(stage, first + step * tiles + i, ROWS, PEERS).astype(BF16) for i in range(tiles)], axis=0
+        )
+
+    conv = dot_nt(eye, rows(0))
+    grad = dot_nt(rev, rows(OWN))
+    ho_ref[0] = (q_ref[0].astype(F32) * conv).astype(BF16)
+    gq_ref[0] = (c_ref[0].astype(F32) * conv).astype(BF16)
+    gk_ref[0] = (grad * v_ref[0].astype(F32)).astype(BF16)
+    gv_ref[0] = (grad * k_ref[0].astype(F32)).astype(BF16)
 
 
 def body(queries, keys, values, cotangent, doc_lengths, filter_taps):
@@ -207,7 +234,7 @@
             pltpu.VMEM((BLOCK, 2 * BLOCK), F32),
             pltpu.SemaphoreType.DMA,
         ],
-        compiler_params=params,
+        compiler_params=pltpu.CompilerParams(vmem_limit_bytes=60 << 20),
         name="pack",
     )(doc_lengths, queries, keys, values, cotangent, filter_taps)
     arrived = lax.all_to_all(packed, ("dp", "ctx"), 0, 0, tiled=True)
@@ -223,10 +250,11 @@
             pltpu.VMEM((DOCS, 2 * BLOCK, BLOCK), BF16),
             pltpu.VMEM((DOCS, BLOCK, BLOCK), BF16),
             pltpu.VMEM((DOCS, 2 * BLOCK, BLOCK), F32),
-            pltpu.VMEM((2 * BLOCK, BLOCKS * BLOCK), BF16),
-            pltpu.VMEM((DOCS, 2 * BLOCK, BLOCK), BF16),
-            pltpu.VMEM((BLOCKS * BLOCK, BLOCK), BF16),
-            pltpu.VMEM((BLOCK, (BLOCKS + 1) * BLOCK), F32),
+            pltpu.VMEM((2, 2 * BLOCK, BLOCKS * BLOCK), BF16),
+            pltpu.VMEM((2, DOCS, 2 * BLOCK, BLOCK), BF16),
+            pltpu.VMEM((2, BLOCKS * BLOCK, BLOCK), BF16),
+            pltpu.VMEM((2, BLOCK, (BLOCKS + 1) * BLOCK), F32),
+            pltpu.VMEM((2, BLOCK, BLOCK), F32),
         ],
         compiler_params=params,
         name="conv",

time: 91.5 us -> 83.2 us (0.909)
  local copies, waits for them, and re-layouts: 6.06 us -> 0.03 us
  Pallas kernels: 25.8 us -> 23.4 us
    unnamed x20 -> x8, local copies, waits for them, and re-layouts: 6.06 us -> 0.03 us
    pallas_call x1, Pallas kernels: 18.6 us -> 15.8 us  [body(): pl.pallas_call(conv_kernel, in_specs=[pl.BlockSpec(memory_space=pltpu.VME...]
where the time goes in v1:
time: 83.2 us; the launch traced here: 82.9 us
  blocking collectives  58.8 us (71%)
  Pallas kernels  23.4 us (28%)
    all_to_all x1, blocking collectives, body(): arrived = lax.all_to_all(packed, ('dp', 'ctx'), 0, 0, tiled=True)  32.9 us
    all_to_all x1, blocking collectives, body(): returned = lax.all_to_all(results, ('dp', 'ctx'), 0, 0, tiled=True)  25.9 us
    pallas_call x1, Pallas kernels, body(): pl.pallas_call(conv_kernel, in_specs=[pl.BlockSpec(memory_space=pltpu.VME...  15.8 us
    pallas_call x1, Pallas kernels, body(): pl.pallas_call(pack_kernel, grid=(steps,), in_specs=[pl.BlockSpec(memory_...  4.7 us
    pallas_call x1, Pallas kernels, body(): pl.pallas_call(finish_kernel, grid=(steps,), in_specs=[tile, tile, tile,...  2.87 us

profile of v1, /device:TPU:0, one launch (start us, length us, event | category | flops | bytes accessed | tf_op | source)
XLA Modules:
  0.0 82.9 jit_solution(10470176284417481245)
XLA Ops:
  0.6 4.7 %pack.1 = bf16[128,40,128]{2,1,0:T(8,128)(2,1)} custom-call(s32[1,4]{1,0:T(1,128)} %len_ref.1, bf16[1,128,2048]{2,1,0:T(8,128)(2,1)} %q_ref.3, bf16[1,128,2048]{2,1,0:T(8,128)(2,1)} %k_ref.3, bf16[1,128,2048]{2,1,0:T(8,128)(2,1)} %v_ref.3, bf16[1,128,2048]{2,1,0:T(8,128)(2,1)} %c_ref.3, f32[128,2048]{1,0:T(8,128)} %filt_hbm.1), custom_call_target="tpu_custom_call" | custom-call | tf_op jit(solution)/shard_map/pack/pallas_call | solution.py:226
  5.3 32.9 %all_to_all.10.in_ref = bf16[128,40,128]{2,1,0:T(8,128)(2,1)S(1)} all-to-all(bf16[128,40,128]{2,1,0:T(8,128)(2,1)} %pack.1), channel_id=1, replica_groups=mesh['dp'=8,'ctx'=16] {'dp','ctx'}, dimensions={0} | all-to-all | bytes 2621440 | tf_op jit(solution)/shard_map/all_to_all | solution.py:240
  38.3 15.8 %conv.1 = bf16[128,40,128]{2,1,0:T(8,128)(2,1)S(1)} custom-call(bf16[128,40,128]{2,1,0:T(8,128)(2,1)S(1)} %all_to_all.10.in_ref), custom_call_target="tpu_custom_call" | custom-call | tf_op jit(solution)/shard_map/conv/pallas_call | solution.py:241
  54.1 0.0 copy-start
  54.1 0.0 copy-start.1
  54.1 0.0 copy-start.2
  54.1 0.0 copy-start.3
  54.1 25.9 %all_to_all.11.in_ref = bf16[128,40,128]{2,1,0:T(8,128)(2,1)S(1)} all-to-all(bf16[128,40,128]{2,1,0:T(8,128)(2,1)S(1)} %conv.1), channel_id=1, replica_groups=mesh['dp'=8,'ctx'=16] {'dp','ctx'}, dimensions={0} | all-to-all | bytes 2621440 | tf_op jit(solution)/shard_map/all_to_all | solution.py:262
  80.0 0.0 copy-done
  80.0 0.0 copy-done.1
  80.0 0.0 copy-done.2
  80.0 0.0 copy-done.3
  80.1 2.9 %finish.1 = (bf16[1,128,2048]{2,1,0:T(8,128)(2,1)}, bf16[1,128,2048]{2,1,0:T(8,128)(2,1)}, bf16[1,128,2048]{2,1,0:T(8,128)(2,1)}, bf16[1,128,2048]{2,1,0:T(8,128)(2,1)}, f32[128,256]{1,0:T(8,128)}) custom-call(bf16[1,128,2048]{2,1,0:T(8,128)(2,1)S(1)} %copy-done, bf16[1,128,2048]{2,1,0:T(8,128)(2,1)S(1)} %copy-done.1, bf16[1,128,2048]{2,1,0:T(8,128)(2,1)S(1)} %copy-done.2, ...), custom_call_target="tpu_custom_call" | custom-call | tf_op jit(solution)/shard_map/finish/pallas_call | solution.py:264
Async XLA Ops:
  54.1 25.9 %copy-start = (bf16[1,128,2048]{2,1,0:T(8,128)(2,1)S(1)}, bf16[1,128,2048]{2,1,0:T(8,128)(2,1)}, u32[]{:S(2)}) copy-start(bf16[1,128,2048]{2,1,0:T(8,128)(2,1)} %q_ref.3) | copy-start | bytes 1572868
  54.1 25.9 %copy-start.1 = (bf16[1,128,2048]{2,1,0:T(8,128)(2,1)S(1)}, bf16[1,128,2048]{2,1,0:T(8,128)(2,1)}, u32[]{:S(2)}) copy-start(bf16[1,128,2048]{2,1,0:T(8,128)(2,1)} %k_ref.3) | copy-start | bytes 1572868
  54.1 25.9 %copy-start.2 = (bf16[1,128,2048]{2,1,0:T(8,128)(2,1)S(1)}, bf16[1,128,2048]{2,1,0:T(8,128)(2,1)}, u32[]{:S(2)}) copy-start(bf16[1,128,2048]{2,1,0:T(8,128)(2,1)} %v_ref.3) | copy-start | bytes 1572868
  54.1 25.9 %copy-start.3 = (bf16[1,128,2048]{2,1,0:T(8,128)(2,1)S(1)}, bf16[1,128,2048]{2,1,0:T(8,128)(2,1)}, u32[]{:S(2)}) copy-start(bf16[1,128,2048]{2,1,0:T(8,128)(2,1)} %c_ref.3) | copy-start | bytes 1572868

commit v2 on v1

--- a/solution.py
+++ b/solution.py
@@ -14,6 +14,8 @@
 OWN = 16
 DOCS = 4
 ROWS = 40
+PITCH = ROWS + 1
+FAR = ROWS * BLOCKS + 1
 FILT, DOC = 2 * OWN, 2 * OWN + 2
 F32, BF16 = jnp.float32, jnp.bfloat16
 
@@ -73,34 +75,34 @@
             end = end + len_ref[0, i]
             doc = doc + (end <= pos).astype(F32)
             doc_rev = doc_rev + (end <= pos_rev).astype(F32)
-        zero = jnp.zeros((8, BLOCK), F32)
         for r in range(PEERS // 8):
-            put(stage, DOC + r * 8 * ROWS, ROWS, doc)
-            put(stage, DOC + 1 + r * 8 * ROWS, ROWS, doc_rev)
-            for extra in range(DOC + 2, ROWS):
-                put(stage, extra + r * 8 * ROWS, ROWS, zero)
+            put(stage, DOC + r * 8 * PITCH, PITCH, doc)
+            put(stage, DOC + 1 + r * 8 * PITCH, PITCH, doc_rev)
 
     gated = dot_tn((k_ref[0].astype(F32) * v_ref[0].astype(F32)).astype(BF16), eye)
     weighted = dot_tn((c_ref[0].astype(F32) * q_ref[0].astype(F32)).astype(BF16), rev)
     for i in range(tiles):
         part = slice(i * BLOCK, (i + 1) * BLOCK)
-        put(stage, step * tiles + i, ROWS, gated[part])
-        put(stage, OWN + step * tiles + i, ROWS, weighted[part])
+        put(stage, step * tiles + i, PITCH, gated[part])
+        put(stage, OWN + step * tiles + i, PITCH, weighted[part])
 
     @pl.when(step == pl.num_programs(0) - 1)
     def _():
         copy.wait()
         lags = dot_tn(filt[...].astype(BF16), eye)
         for i in range(2):
-            put(stage, FILT + i, ROWS, lags[i * BLOCK : (i + 1) * BLOCK])
-        out_ref[...] = stage[...].reshape(PEERS, ROWS, BLOCK).astype(BF16)
+            put(stage, FILT + i, PITCH, lags[i * BLOCK : (i + 1) * BLOCK])
+        for r in range(PEERS):
+            out_ref[r] = stage[r * PITCH : r * PITCH + ROWS, :].astype(BF16)
 
 
 def conv_kernel(in_ref, out_ref, src, dst, mask, rel, rel_t, keep, stack, extra, taps, cross, fold):
     row, col = iota(0), iota(1)
-    far = ROWS * BLOCKS
-    src[...] = in_ref[...].astype(F32).reshape(PEERS * ROWS, BLOCK)
-    dst[...] = jnp.zeros_like(dst)
+    far = FAR
+    for i in range(SEQS):
+        src[i * FAR : i * FAR + FAR - 1, :] = (
+            in_ref[i * BLOCKS : (i + 1) * BLOCKS].astype(F32).reshape(FAR - 1, BLOCK)
+        )
     stack[...] = jnp.zeros_like(stack)
     cross[...] = jnp.zeros_like(cross)
 
@@ -143,16 +145,29 @@
             before = turned
 
     def multiply(t, slot):
-        out = keep[0] * dot(stack[slot], taps[slot])
+        parts = []
+        for g in range(4):
+            lanes = slice(512 * g, 512 * g + 512)
+            rows = jnp.concatenate([stack[slot, 32 * g : BLOCK, lanes], stack[slot, BLOCK + 32 * g :, lanes]], axis=0)
+            parts.append(dot(rows, taps[slot, lanes, :]))
+        total = []
+        for way in range(2):
+            for g in range(4):
+                at = [way * (BLOCK - 32 * i) + 32 * (g - i) for i in range(g + 1)]
+                total.append(sum(parts[i][at[i] : at[i] + 32] for i in range(g + 1)))
+        out = keep[0] * jnp.concatenate(total, axis=0)
         for k in range(1, DOCS):
             out = out + keep[k] * dot(extra[slot, k], taps[slot, :BLOCK])
         for b in range(BLOCKS):
             dst[pl.ds(b * ROWS + t, 8, stride=far), :] = out[8 * b : 8 * b + 8]
             dst[pl.ds((BLOCKS - 1 - b) * ROWS + OWN + t, 8, stride=far), :] = out[BLOCK + 8 * b : BLOCK + 8 * b + 8]
         wt = jnp.transpose(blocks(OWN + t)).astype(BF16)
-        cross[slot, :, : BLOCKS * BLOCK] = dot(wt * rel_t[0], stack[slot, :BLOCK, :])
-        for k in range(1, DOCS):
-            cross[slot, :, :BLOCK] += dot(wt * rel_t[k], extra[slot, k, :BLOCK, :])
+        heads = wt * rel_t[0]
+        cross[slot, :, BLOCK : BLOCKS * BLOCK] = dot(heads, stack[slot, :BLOCK, BLOCK:])
+        cross[slot, :, :BLOCK] = dot(
+            jnp.concatenate([heads] + [wt * rel_t[k] for k in range(1, DOCS)], axis=1),
+            jnp.concatenate([stack[slot, :BLOCK, :BLOCK]] + [extra[slot, k, :BLOCK, :] for k in range(1, DOCS)], axis=0),
+        )
 
     def gather(t, slot):
         line = (t // 2) * far + FILT + t % 2
@@ -166,8 +181,8 @@
                 sums[d] += pltpu.roll(jnp.where(lower, here, there), 8 * k + 1, 1, stride=1, stride_axis=0)
                 here = there
         for d in range(BLOCKS):
-            fold[slot, 8 * d : 8 * d + 8, :] = sums[d]
-        grad = sum(fold[slot, pl.ds(i, BLOCKS, stride=8), :] for i in range(8))
+            fold[slot, 9 * d : 9 * d + 8, :] = sums[d]
+        grad = sum(take(fold.at[slot], i, 9, BLOCKS) for i in range(8))
         high = grad.astype(BF16).astype(F32)
         put(dst, line, ROWS, high)
         put(dst, line + 2, ROWS, grad - high)
@@ -186,7 +201,10 @@
 
     lax.fori_loop(0, OWN // 2, pair, 0)
     gather(OWN - 1, 1)
-    out_ref[...] = dst[...].reshape(PEERS, ROWS, BLOCK).astype(BF16)
+    for i in range(SEQS):
+        out_ref[i * BLOCKS : (i + 1) * BLOCKS] = (
+            dst[i * FAR : i * FAR + FAR - 1, :].reshape(BLOCKS, ROWS, BLOCK).astype(BF16)
+        )
 
 
 def finish_kernel(q_ref, k_ref, v_ref, c_ref, in_ref, ho_ref, gq_ref, gk_ref, gv_ref, gf_ref, stage):
@@ -196,16 +214,17 @@
 
     @pl.when(step == 0)
     def _():
-        stage[...] = in_ref[...].astype(F32).reshape(PEERS * ROWS, BLOCK)
+        for r in range(PEERS):
+            stage[r * PITCH : r * PITCH + ROWS, :] = in_ref[r].astype(F32)
         turn = ((iota(0) + iota(1)) % BLOCK == 0).astype(F32).astype(BF16)
         for i in range(2):
-            high = take(stage, FILT + i, ROWS, PEERS).astype(BF16)
-            low = take(stage, FILT + 2 + i, ROWS, PEERS).astype(BF16)
+            high = take(stage, FILT + i, PITCH, PEERS).astype(BF16)
+            low = take(stage, FILT + 2 + i, PITCH, PEERS).astype(BF16)
             gf_ref[:, i * BLOCK : (i + 1) * BLOCK] = dot_nt(turn, high) + dot_nt(turn, low)
 
     def rows(first):
         return jnp.concatenate(
-            [take(stage, first + step * tiles + i, ROWS, PEERS).astype(BF16) for i in range(tiles)], axis=0
+            [take(stage, first + step * tiles + i, PITCH, PEERS).astype(BF16) for i in range(tiles)], axis=0
         )
 
     conv = dot_nt(eye, rows(0))
@@ -230,7 +249,7 @@
         out_specs=whole,
         out_shape=message,
         scratch_shapes=[
-            pltpu.VMEM((PEERS * ROWS, BLOCK), F32),
+            pltpu.VMEM((PEERS * PITCH, BLOCK), F32),
             pltpu.VMEM((BLOCK, 2 * BLOCK), F32),
             pltpu.SemaphoreType.DMA,
         ],
@@ -244,8 +263,8 @@
         out_specs=pl.BlockSpec(memory_space=pltpu.VMEM),
         out_shape=message,
         scratch_shapes=[
-            pltpu.VMEM((PEERS * ROWS, BLOCK), F32),
-            pltpu.VMEM((PEERS * ROWS, BLOCK), F32),
+            pltpu.VMEM((SEQS * FAR, BLOCK), F32),
+            pltpu.VMEM((SEQS * FAR, BLOCK), F32),
             pltpu.VMEM((2 * BLOCK, BLOCKS * BLOCK), BF16),
             pltpu.VMEM((DOCS, 2 * BLOCK, BLOCK), BF16),
             pltpu.VMEM((DOCS, BLOCK, BLOCK), BF16),
@@ -254,7 +273,7 @@
             pltpu.VMEM((2, DOCS, 2 * BLOCK, BLOCK), BF16),
             pltpu.VMEM((2, BLOCKS * BLOCK, BLOCK), BF16),
             pltpu.VMEM((2, BLOCK, (BLOCKS + 1) * BLOCK), F32),
-            pltpu.VMEM((2, BLOCK, BLOCK), F32),
+            pltpu.VMEM((2, 9 * BLOCKS, BLOCK), F32),
         ],
         compiler_params=params,
         name="conv",
@@ -267,7 +286,7 @@
         in_specs=[tile, tile, tile, tile, whole],
         out_specs=[tile, tile, tile, tile, pl.BlockSpec((BLOCK, 2 * BLOCK), lambda i: (0, 0))],
         out_shape=[row_out, row_out, row_out, row_out, jax.ShapeDtypeStruct((BLOCK, 2 * BLOCK), F32)],
-        scratch_shapes=[pltpu.VMEM((PEERS * ROWS, BLOCK), F32)],
+        scratch_shapes=[pltpu.VMEM((PEERS * PITCH, BLOCK), F32)],
         compiler_params=params,
         name="finish",
     )(queries, keys, values, cotangent, returned)

time: 83.2 us -> 79.6 us (0.957)
  Pallas kernels: 23.4 us -> 19.8 us
    pallas_call x1, Pallas kernels: 15.8 us -> 12.5 us  [body(): pl.pallas_call(conv_kernel, in_specs=[pl.BlockSpec(memory_space=pltpu.VME...]
where the time goes in v2:
time: 79.6 us; the launch traced here: 79.4 us
  blocking collectives  58.8 us (74%)
  Pallas kernels  19.8 us (25%)
    all_to_all x1, blocking collectives, body(): arrived = lax.all_to_all(packed, ('dp', 'ctx'), 0, 0, tiled=True)  32.9 us
    all_to_all x1, blocking collectives, body(): returned = lax.all_to_all(results, ('dp', 'ctx'), 0, 0, tiled=True)  25.9 us
    pallas_call x1, Pallas kernels, body(): pl.pallas_call(conv_kernel, in_specs=[pl.BlockSpec(memory_space=pltpu.VME...  12.5 us
    pallas_call x1, Pallas kernels, body(): pl.pallas_call(pack_kernel, grid=(steps,), in_specs=[pl.BlockSpec(memory_...  4.51 us
    pallas_call x1, Pallas kernels, body(): pl.pallas_call(finish_kernel, grid=(steps,), in_specs=[tile, tile, tile,...  2.84 us

profile of v2, /device:TPU:0, one launch (start us, length us, event | category | flops | bytes accessed | tf_op | source)
XLA Modules:
  0.0 79.4 jit_solution(17087951152258927309)
XLA Ops:
  0.6 4.5 %pack.1 = bf16[128,40,128]{2,1,0:T(8,128)(2,1)} custom-call(s32[1,4]{1,0:T(1,128)} %len_ref.1, bf16[1,128,2048]{2,1,0:T(8,128)(2,1)} %q_ref.3, bf16[1,128,2048]{2,1,0:T(8,128)(2,1)} %k_ref.3, bf16[1,128,2048]{2,1,0:T(8,128)(2,1)} %v_ref.3, bf16[1,128,2048]{2,1,0:T(8,128)(2,1)} %c_ref.3, f32[128,2048]{1,0:T(8,128)} %filt_hbm.1), custom_call_target="tpu_custom_call" | custom-call | tf_op jit(solution)/shard_map/pack/pallas_call | solution.py:245
  5.1 32.9 %all_to_all.10.in_ref = bf16[128,40,128]{2,1,0:T(8,128)(2,1)S(1)} all-to-all(bf16[128,40,128]{2,1,0:T(8,128)(2,1)} %pack.1), channel_id=1, replica_groups=mesh['dp'=8,'ctx'=16] {'dp','ctx'}, dimensions={0} | all-to-all | bytes 2621440 | tf_op jit(solution)/shard_map/all_to_all | solution.py:259
  38.1 12.5 %conv.1 = bf16[128,40,128]{2,1,0:T(8,128)(2,1)S(1)} custom-call(bf16[128,40,128]{2,1,0:T(8,128)(2,1)S(1)} %all_to_all.10.in_ref), custom_call_target="tpu_custom_call" | custom-call | tf_op jit(solution)/shard_map/conv/pallas_call | solution.py:260
  50.6 0.0 copy-start
  50.6 0.0 copy-start.1
  50.6 0.0 copy-start.2
  50.6 0.0 copy-start.3
  50.6 25.9 %all_to_all.11.in_ref = bf16[128,40,128]{2,1,0:T(8,128)(2,1)S(1)} all-to-all(bf16[128,40,128]{2,1,0:T(8,128)(2,1)S(1)} %conv.1), channel_id=1, replica_groups=mesh['dp'=8,'ctx'=16] {'dp','ctx'}, dimensions={0} | all-to-all | bytes 2621440 | tf_op jit(solution)/shard_map/all_to_all | solution.py:281
  76.5 0.0 copy-done
  76.5 0.0 copy-done.1
  76.5 0.0 copy-done.2
  76.5 0.0 copy-done.3
  76.5 2.8 %finish.1 = (bf16[1,128,2048]{2,1,0:T(8,128)(2,1)}, bf16[1,128,2048]{2,1,0:T(8,128)(2,1)}, bf16[1,128,2048]{2,1,0:T(8,128)(2,1)}, bf16[1,128,2048]{2,1,0:T(8,128)(2,1)}, f32[128,256]{1,0:T(8,128)}) custom-call(bf16[1,128,2048]{2,1,0:T(8,128)(2,1)S(1)} %copy-done, bf16[1,128,2048]{2,1,0:T(8,128)(2,1)S(1)} %copy-done.1, bf16[1,128,2048]{2,1,0:T(8,128)(2,1)S(1)} %copy-done.2, ...), custom_call_target="tpu_custom_call" | custom-call | tf_op jit(solution)/shard_map/finish/pallas_call | solution.py:283
Async XLA Ops:
  50.6 25.9 %copy-start = (bf16[1,128,2048]{2,1,0:T(8,128)(2,1)S(1)}, bf16[1,128,2048]{2,1,0:T(8,128)(2,1)}, u32[]{:S(2)}) copy-start(bf16[1,128,2048]{2,1,0:T(8,128)(2,1)} %q_ref.3) | copy-start | bytes 1572868
  50.6 25.9 %copy-start.1 = (bf16[1,128,2048]{2,1,0:T(8,128)(2,1)S(1)}, bf16[1,128,2048]{2,1,0:T(8,128)(2,1)}, u32[]{:S(2)}) copy-start(bf16[1,128,2048]{2,1,0:T(8,128)(2,1)} %k_ref.3) | copy-start | bytes 1572868
  50.6 25.9 %copy-start.2 = (bf16[1,128,2048]{2,1,0:T(8,128)(2,1)S(1)}, bf16[1,128,2048]{2,1,0:T(8,128)(2,1)}, u32[]{:S(2)}) copy-start(bf16[1,128,2048]{2,1,0:T(8,128)(2,1)} %v_ref.3) | copy-start | bytes 1572868
  50.6 25.9 %copy-start.3 = (bf16[1,128,2048]{2,1,0:T(8,128)(2,1)S(1)}, bf16[1,128,2048]{2,1,0:T(8,128)(2,1)}, u32[]{:S(2)}) copy-start(bf16[1,128,2048]{2,1,0:T(8,128)(2,1)} %c_ref.3) | copy-start | bytes 1572868

commit v3 on v2

--- a/solution.py
+++ b/solution.py
@@ -13,6 +13,7 @@
 PEERS = SEQS * BLOCKS
 OWN = 16
 DOCS = 4
+CHUNKS = 2
 ROWS = 40
 PITCH = ROWS + 1
 FAR = ROWS * BLOCKS + 1
@@ -52,48 +53,55 @@
     )
 
 
-def pack_kernel(len_ref, q_ref, k_ref, v_ref, c_ref, filt_hbm, out_ref, stage, filt, sem):
-    step = pl.program_id(0)
-    tiles = q_ref.shape[2] // BLOCK
+def pack_kernel(len_ref, q_hbm, k_hbm, v_hbm, c_hbm, filt_hbm, out_ref, stage, held, filt, sems, filt_sem):
+    width = held.shape[2] // CHUNKS
     eye, rev = eye_rev()
+    copies = [
+        [
+            pltpu.make_async_copy(
+                hbm.at[0, :, pl.ds(n * width, width)], held.at[i, :, pl.ds(n * width, width)], sems.at[n, i]
+            )
+            for i, hbm in enumerate((k_hbm, v_hbm, c_hbm, q_hbm))
+        ]
+        for n in range(CHUNKS)
+    ]
     copy = pltpu.make_async_copy(
-        filt_hbm.at[:, pl.ds(pl.multiple_of(lax.axis_index("dp") * 2 * BLOCK, BLOCK), 2 * BLOCK)],
-        filt,
-        sem,
+        filt_hbm.at[:, pl.ds(pl.multiple_of(lax.axis_index("dp") * 2 * BLOCK, BLOCK), 2 * BLOCK)], filt, filt_sem
     )
-
-    @pl.when(step == 0)
-    def _():
-        copy.start()
-        lane = iota(1, (8, BLOCK))
-        pos = lax.axis_index("ctx") * BLOCK + lane
-        pos_rev = lax.axis_index("ctx") * BLOCK + BLOCK - 1 - lane
-        doc = jnp.zeros((8, BLOCK), F32)
-        doc_rev = jnp.zeros((8, BLOCK), F32)
-        end = jnp.int32(0)
-        for i in range(DOCS):
-            end = end + len_ref[0, i]
-            doc = doc + (end <= pos).astype(F32)
-            doc_rev = doc_rev + (end <= pos_rev).astype(F32)
-        for r in range(PEERS // 8):
-            put(stage, DOC + r * 8 * PITCH, PITCH, doc)
-            put(stage, DOC + 1 + r * 8 * PITCH, PITCH, doc_rev)
-
-    gated = dot_tn((k_ref[0].astype(F32) * v_ref[0].astype(F32)).astype(BF16), eye)
-    weighted = dot_tn((c_ref[0].astype(F32) * q_ref[0].astype(F32)).astype(BF16), rev)
-    for i in range(tiles):
-        part = slice(i * BLOCK, (i + 1) * BLOCK)
-        put(stage, step * tiles + i, PITCH, gated[part])
-        put(stage, OWN + step * tiles + i, PITCH, weighted[part])
-
-    @pl.when(step == pl.num_programs(0) - 1)
-    def _():
-        copy.wait()
-        lags = dot_tn(filt[...].astype(BF16), eye)
-        for i in range(2):
-            put(stage, FILT + i, PITCH, lags[i * BLOCK : (i + 1) * BLOCK])
-        for r in range(PEERS):
-            out_ref[r] = stage[r * PITCH : r * PITCH + ROWS, :].astype(BF16)
+    for four in copies:
+        for one in four:
+            one.start()
+    copy.start()
+    lane = iota(1, (8, BLOCK))
+    pos = lax.axis_index("ctx") * BLOCK + lane
+    pos_rev = lax.axis_index("ctx") * BLOCK + BLOCK - 1 - lane
+    doc = jnp.zeros((8, BLOCK), F32)
+    doc_rev = jnp.zeros((8, BLOCK), F32)
+    end = jnp.int32(0)
+    for i in range(DOCS):
+        end = end + len_ref[0, i]
+        doc = doc + (end <= pos).astype(F32)
+        doc_rev = doc_rev + (end <= pos_rev).astype(F32)
+    for r in range(PEERS // 8):
+        put(stage, DOC + r * 8 * PITCH, PITCH, doc)
+        put(stage, DOC + 1 + r * 8 * PITCH, PITCH, doc_rev)
+    for n, four in enumerate(copies):
+        for one in four:
+            one.wait()
+        lanes = slice(n * width, (n + 1) * width)
+        key, value, cot, query = (held[i, :, lanes].astype(F32) for i in range(4))
+        gated = dot_tn((key * value).astype(BF16), eye)
+        weighted = dot_tn((cot * query).astype(BF16), rev)
+        for i in range(width // BLOCK):
+            part = slice(i * BLOCK, (i + 1) * BLOCK)
+            put(stage, n * (width // BLOCK) + i, PITCH, gated[part])
+            put(stage, OWN + n * (width // BLOCK) + i, PITCH, weighted[part])
+    copy.wait()
+    lags = dot_tn(filt[...].astype(BF16), eye)
+    for i in range(2):
+        put(stage, FILT + i, PITCH, lags[i * BLOCK : (i + 1) * BLOCK])
+    for r in range(PEERS):
+        out_ref[r] = stage[r * PITCH : r * PITCH + ROWS, :].astype(BF16)
 
 
 def conv_kernel(in_ref, out_ref, src, dst, mask, rel, rel_t, keep, stack, extra, taps, cross, fold):
@@ -191,12 +199,12 @@
 
     def pair(u, carry):
         t = 2 * u
+        gather(jnp.maximum(t - 1, 0), 1)
         multiply(t, 0)
         build(t + 1, 1)
-        gather(jnp.maximum(t - 1, 0), 1)
+        gather(t, 0)
         multiply(t + 1, 1)
         build(jnp.minimum(t + 2, OWN - 1), 0)
-        gather(t, 0)
         return carry
 
     lax.fori_loop(0, OWN // 2, pair, 0)
@@ -236,7 +244,7 @@
 
 
 def body(queries, keys, values, cotangent, doc_lengths, filter_taps):
-    width = 512
+    width = 2048
     steps = queries.shape[2] // width
     tile = pl.BlockSpec((1, BLOCK, width), lambda i: (0, 0, i))
     whole = pl.BlockSpec((PEERS, ROWS, BLOCK), lambda i: (0, 0, 0))
@@ -244,13 +252,14 @@
     params = pltpu.CompilerParams(vmem_limit_bytes=32 << 20)
     packed = pl.pallas_call(
         pack_kernel,
-        grid=(steps,),
-        in_specs=[pl.BlockSpec(memory_space=pltpu.SMEM), tile, tile, tile, tile, pl.BlockSpec(memory_space=pl.ANY)],
-        out_specs=whole,
+        in_specs=[pl.BlockSpec(memory_space=pltpu.SMEM)] + [pl.BlockSpec(memory_space=pltpu.HBM)] * 5,
+        out_specs=pl.BlockSpec(memory_space=pltpu.VMEM),
         out_shape=message,
         scratch_shapes=[
             pltpu.VMEM((PEERS * PITCH, BLOCK), F32),
+            pltpu.VMEM((4,) + queries.shape[1:], BF16),
             pltpu.VMEM((BLOCK, 2 * BLOCK), F32),
+            pltpu.SemaphoreType.DMA((CHUNKS, 4)),
             pltpu.SemaphoreType.DMA,
         ],
         compiler_params=pltpu.CompilerParams(vmem_limit_bytes=60 << 20),

time: 79.6 us -> 77 us (0.967)
  Pallas kernels: 19.8 us -> 17.2 us
    pallas_call x1, Pallas kernels: 12.5 us -> 11.2 us  [body(): pl.pallas_call(conv_kernel, in_specs=[pl.BlockSpec(memory_space=pltpu.VME...]
    pallas_call x1, Pallas kernels: 2.84 us -> 1.97 us  [body(): pl.pallas_call(finish_kernel, grid=(steps,), in_specs=[tile, tile, tile,...]
where the time goes in v3:
time: 77 us; the launch traced here: 76.7 us
  blocking collectives  58.8 us (76%)
  Pallas kernels  17.2 us (22%)
    all_to_all x1, blocking collectives, body(): arrived = lax.all_to_all(packed, ('dp', 'ctx'), 0, 0, tiled=True)  32.9 us
    all_to_all x1, blocking collectives, body(): returned = lax.all_to_all(results, ('dp', 'ctx'), 0, 0, tiled=True)  25.9 us
    pallas_call x1, Pallas kernels, body(): pl.pallas_call(conv_kernel, in_specs=[pl.BlockSpec(memory_space=pltpu.VME...  11.2 us
    pallas_call x1, Pallas kernels, body(): pl.pallas_call(pack_kernel, in_specs=[pl.BlockSpec(memory_space=pltpu.SME...  4.03 us
    pallas_call x1, Pallas kernels, body(): pl.pallas_call(finish_kernel, grid=(steps,), in_specs=[tile, tile, tile,...  1.97 us

profile of v3, /device:TPU:0, one launch (start us, length us, event | category | flops | bytes accessed | tf_op | source)
XLA Modules:
  0.0 76.7 jit_solution(6223193708735117468)
XLA Ops:
  0.6 4.0 %pack.1 = bf16[128,40,128]{2,1,0:T(8,128)(2,1)} custom-call(s32[1,4]{1,0:T(1,128)} %len_ref.1, bf16[1,128,2048]{2,1,0:T(8,128)(2,1)} %q_ref.1, bf16[1,128,2048]{2,1,0:T(8,128)(2,1)} %k_ref.1, bf16[1,128,2048]{2,1,0:T(8,128)(2,1)} %v_ref.1, bf16[1,128,2048]{2,1,0:T(8,128)(2,1)} %c_ref.1, f32[128,2048]{1,0:T(8,128)} %filt_hbm.1), custom_call_target="tpu_custom_call" | custom-call | tf_op jit(solution)/shard_map/pack/pallas_call | solution.py:253
  4.7 32.9 %all_to_all.10.in_ref = bf16[128,40,128]{2,1,0:T(8,128)(2,1)S(1)} all-to-all(bf16[128,40,128]{2,1,0:T(8,128)(2,1)} %pack.1), channel_id=1, replica_groups=mesh['dp'=8,'ctx'=16] {'dp','ctx'}, dimensions={0} | all-to-all | bytes 2621440 | tf_op jit(solution)/shard_map/all_to_all | solution.py:268
  37.6 11.2 %conv.1 = bf16[128,40,128]{2,1,0:T(8,128)(2,1)S(1)} custom-call(bf16[128,40,128]{2,1,0:T(8,128)(2,1)S(1)} %all_to_all.10.in_ref), custom_call_target="tpu_custom_call" | custom-call | tf_op jit(solution)/shard_map/conv/pallas_call | solution.py:269
  48.8 0.0 copy-start
  48.8 0.0 copy-start.1
  48.8 0.0 copy-start.2
  48.9 0.0 copy-start.3
  48.9 25.9 %all_to_all.11.in_ref = bf16[128,40,128]{2,1,0:T(8,128)(2,1)S(1)} all-to-all(bf16[128,40,128]{2,1,0:T(8,128)(2,1)S(1)} %conv.1), channel_id=1, replica_groups=mesh['dp'=8,'ctx'=16] {'dp','ctx'}, dimensions={0} | all-to-all | bytes 2621440 | tf_op jit(solution)/shard_map/all_to_all | solution.py:290
  74.8 0.0 copy-done
  74.8 0.0 copy-done.1
  74.8 0.0 copy-done.2
  74.8 0.0 copy-done.3
  74.8 2.0 %finish.1 = (bf16[1,128,2048]{2,1,0:T(8,128)(2,1)}, bf16[1,128,2048]{2,1,0:T(8,128)(2,1)}, bf16[1,128,2048]{2,1,0:T(8,128)(2,1)}, bf16[1,128,2048]{2,1,0:T(8,128)(2,1)}, f32[128,256]{1,0:T(8,128)}) custom-call(bf16[1,128,2048]{2,1,0:T(8,128)(2,1)S(1)} %copy-done, bf16[1,128,2048]{2,1,0:T(8,128)(2,1)S(1)} %copy-done.1, bf16[1,128,2048]{2,1,0:T(8,128)(2,1)S(1)} %copy-done.2, ...), custom_call_target="tpu_custom_call" | custom-call | tf_op jit(solution)/shard_map/finish/pallas_call | solution.py:292
Async XLA Ops:
  48.8 25.9 %copy-start = (bf16[1,128,2048]{2,1,0:T(8,128)(2,1)S(1)}, bf16[1,128,2048]{2,1,0:T(8,128)(2,1)}, u32[]{:S(2)}) copy-start(bf16[1,128,2048]{2,1,0:T(8,128)(2,1)} %q_ref.1) | copy-start | bytes 1572868
  48.8 25.9 %copy-start.1 = (bf16[1,128,2048]{2,1,0:T(8,128)(2,1)S(1)}, bf16[1,128,2048]{2,1,0:T(8,128)(2,1)}, u32[]{:S(2)}) copy-start(bf16[1,128,2048]{2,1,0:T(8,128)(2,1)} %k_ref.1) | copy-start | bytes 1572868
  48.8 25.9 %copy-start.2 = (bf16[1,128,2048]{2,1,0:T(8,128)(2,1)S(1)}, bf16[1,128,2048]{2,1,0:T(8,128)(2,1)}, u32[]{:S(2)}) copy-start(bf16[1,128,2048]{2,1,0:T(8,128)(2,1)} %v_ref.1) | copy-start | bytes 1572868
  48.9 25.9 %copy-start.3 = (bf16[1,128,2048]{2,1,0:T(8,128)(2,1)S(1)}, bf16[1,128,2048]{2,1,0:T(8,128)(2,1)}, u32[]{:S(2)}) copy-start(bf16[1,128,2048]{2,1,0:T(8,128)(2,1)} %c_ref.1) | copy-start | bytes 1572868

commit v4 on v3

--- a/solution.py
+++ b/solution.py
@@ -53,7 +53,7 @@
     )
 
 
-def pack_kernel(len_ref, q_hbm, k_hbm, v_hbm, c_hbm, filt_hbm, out_ref, stage, held, filt, sems, filt_sem):
+def pack_kernel(len_ref, q_hbm, k_hbm, v_hbm, c_hbm, filt_hbm, out_hbm, stage, held, filt, ready, sems, filt_sem, out_sems):
     width = held.shape[2] // CHUNKS
     eye, rev = eye_rev()
     copies = [
@@ -100,8 +100,16 @@
     lags = dot_tn(filt[...].astype(BF16), eye)
     for i in range(2):
         put(stage, FILT + i, PITCH, lags[i * BLOCK : (i + 1) * BLOCK])
-    for r in range(PEERS):
-        out_ref[r] = stage[r * PITCH : r * PITCH + ROWS, :].astype(BF16)
+    share = PEERS // 4
+    leaving = []
+    for n in range(4):
+        for r in range(n * share, (n + 1) * share):
+            ready[r] = stage[r * PITCH : r * PITCH + ROWS, :].astype(BF16)
+        part = pl.ds(n * share, share)
+        leaving.append(pltpu.make_async_copy(ready.at[part], out_hbm.at[part], out_sems.at[n]))
+        leaving[n].start()
+    for one in leaving:
+        one.wait()
 
 
 def conv_kernel(in_ref, out_ref, src, dst, mask, rel, rel_t, keep, stack, extra, taps, cross, fold):
@@ -169,6 +177,8 @@
         for b in range(BLOCKS):
             dst[pl.ds(b * ROWS + t, 8, stride=far), :] = out[8 * b : 8 * b + 8]
             dst[pl.ds((BLOCKS - 1 - b) * ROWS + OWN + t, 8, stride=far), :] = out[BLOCK + 8 * b : BLOCK + 8 * b + 8]
+
+    def correlate(t, slot):
         wt = jnp.transpose(blocks(OWN + t)).astype(BF16)
         heads = wt * rel_t[0]
         cross[slot, :, BLOCK : BLOCKS * BLOCK] = dot(heads, stack[slot, :BLOCK, BLOCK:])
@@ -199,11 +209,13 @@
 
     def pair(u, carry):
         t = 2 * u
+        multiply(t, 0)
         gather(jnp.maximum(t - 1, 0), 1)
-        multiply(t, 0)
+        correlate(t, 0)
         build(t + 1, 1)
+        multiply(t + 1, 1)
         gather(t, 0)
-        multiply(t + 1, 1)
+        correlate(t + 1, 1)
         build(jnp.minimum(t + 2, OWN - 1), 0)
         return carry
 
@@ -253,14 +265,16 @@
     packed = pl.pallas_call(
         pack_kernel,
         in_specs=[pl.BlockSpec(memory_space=pltpu.SMEM)] + [pl.BlockSpec(memory_space=pltpu.HBM)] * 5,
-        out_specs=pl.BlockSpec(memory_space=pltpu.VMEM),
+        out_specs=pl.BlockSpec(memory_space=pl.ANY),
         out_shape=message,
         scratch_shapes=[
             pltpu.VMEM((PEERS * PITCH, BLOCK), F32),
             pltpu.VMEM((4,) + queries.shape[1:], BF16),
             pltpu.VMEM((BLOCK, 2 * BLOCK), F32),
+            pltpu.VMEM((PEERS, ROWS, BLOCK), BF16),
             pltpu.SemaphoreType.DMA((CHUNKS, 4)),
             pltpu.SemaphoreType.DMA,
+            pltpu.SemaphoreType.DMA((4,)),
         ],
         compiler_params=pltpu.CompilerParams(vmem_limit_bytes=60 << 20),
         name="pack",

time: 77 us -> 76.9 us (level)
  no operation moved by 1% of the time
where the time goes in v4:
time: 76.9 us; the launch traced here: 76.7 us
  blocking collectives  58.8 us (76%)
  Pallas kernels  17.1 us (22%)
    all_to_all x1, blocking collectives, body(): arrived = lax.all_to_all(packed, ('dp', 'ctx'), 0, 0, tiled=True)  32.9 us
    all_to_all x1, blocking collectives, body(): returned = lax.all_to_all(results, ('dp', 'ctx'), 0, 0, tiled=True)  25.9 us
    pallas_call x1, Pallas kernels, body(): pl.pallas_call(conv_kernel, in_specs=[pl.BlockSpec(memory_space=pltpu.VME...  11.2 us
    pallas_call x1, Pallas kernels, body(): pl.pallas_call(pack_kernel, in_specs=[pl.BlockSpec(memory_space=pltpu.SME...  3.99 us
    pallas_call x1, Pallas kernels, body(): pl.pallas_call(finish_kernel, grid=(steps,), in_specs=[tile, tile, tile,...  1.97 us

profile of v4, /device:TPU:0, one launch (start us, length us, event | category | flops | bytes accessed | tf_op | source)
XLA Modules:
  0.0 76.7 jit_solution(930070703958874000)
XLA Ops:
  0.6 4.0 %pack.1 = bf16[128,40,128]{2,1,0:T(8,128)(2,1)} custom-call(s32[1,4]{1,0:T(1,128)} %len_ref.1, bf16[1,128,2048]{2,1,0:T(8,128)(2,1)} %q_ref.1, bf16[1,128,2048]{2,1,0:T(8,128)(2,1)} %k_ref.1, bf16[1,128,2048]{2,1,0:T(8,128)(2,1)} %v_ref.1, bf16[1,128,2048]{2,1,0:T(8,128)(2,1)} %c_ref.1, f32[128,2048]{1,0:T(8,128)} %filt_hbm.1), custom_call_target="tpu_custom_call" | custom-call | tf_op jit(solution)/shard_map/pack/pallas_call | solution.py:265
  4.6 32.9 %all_to_all.10.in_ref = bf16[128,40,128]{2,1,0:T(8,128)(2,1)S(1)} all-to-all(bf16[128,40,128]{2,1,0:T(8,128)(2,1)} %pack.1), channel_id=1, replica_groups=mesh['dp'=8,'ctx'=16] {'dp','ctx'}, dimensions={0} | all-to-all | bytes 2621440 | tf_op jit(solution)/shard_map/all_to_all | solution.py:282
  37.6 11.2 %conv.1 = bf16[128,40,128]{2,1,0:T(8,128)(2,1)S(1)} custom-call(bf16[128,40,128]{2,1,0:T(8,128)(2,1)S(1)} %all_to_all.10.in_ref), custom_call_target="tpu_custom_call" | custom-call | tf_op jit(solution)/shard_map/conv/pallas_call | solution.py:283
  48.7 0.0 copy-start
  48.8 0.0 copy-start.1
  48.8 0.0 copy-start.2
  48.8 0.0 copy-start.3
  48.8 25.9 %all_to_all.11.in_ref = bf16[128,40,128]{2,1,0:T(8,128)(2,1)S(1)} all-to-all(bf16[128,40,128]{2,1,0:T(8,128)(2,1)S(1)} %conv.1), channel_id=1, replica_groups=mesh['dp'=8,'ctx'=16] {'dp','ctx'}, dimensions={0} | all-to-all | bytes 2621440 | tf_op jit(solution)/shard_map/all_to_all | solution.py:304
  74.7 0.0 copy-done
  74.7 0.0 copy-done.1
  74.7 0.0 copy-done.2
  74.7 0.0 copy-done.3
  74.7 2.0 %finish.1 = (bf16[1,128,2048]{2,1,0:T(8,128)(2,1)}, bf16[1,128,2048]{2,1,0:T(8,128)(2,1)}, bf16[1,128,2048]{2,1,0:T(8,128)(2,1)}, bf16[1,128,2048]{2,1,0:T(8,128)(2,1)}, f32[128,256]{1,0:T(8,128)}) custom-call(bf16[1,128,2048]{2,1,0:T(8,128)(2,1)S(1)} %copy-done, bf16[1,128,2048]{2,1,0:T(8,128)(2,1)S(1)} %copy-done.1, bf16[1,128,2048]{2,1,0:T(8,128)(2,1)S(1)} %copy-done.2, ...), custom_call_target="tpu_custom_call" | custom-call | tf_op jit(solution)/shard_map/finish/pallas_call | solution.py:306
Async XLA Ops:
  48.7 25.9 %copy-start = (bf16[1,128,2048]{2,1,0:T(8,128)(2,1)S(1)}, bf16[1,128,2048]{2,1,0:T(8,128)(2,1)}, u32[]{:S(2)}) copy-start(bf16[1,128,2048]{2,1,0:T(8,128)(2,1)} %q_ref.1) | copy-start | bytes 1572868
  48.8 25.9 %copy-start.1 = (bf16[1,128,2048]{2,1,0:T(8,128)(2,1)S(1)}, bf16[1,128,2048]{2,1,0:T(8,128)(2,1)}, u32[]{:S(2)}) copy-start(bf16[1,128,2048]{2,1,0:T(8,128)(2,1)} %k_ref.1) | copy-start | bytes 1572868
  48.8 25.9 %copy-start.2 = (bf16[1,128,2048]{2,1,0:T(8,128)(2,1)S(1)}, bf16[1,128,2048]{2,1,0:T(8,128)(2,1)}, u32[]{:S(2)}) copy-start(bf16[1,128,2048]{2,1,0:T(8,128)(2,1)} %v_ref.1) | copy-start | bytes 1572868
  48.8 25.9 %copy-start.3 = (bf16[1,128,2048]{2,1,0:T(8,128)(2,1)S(1)}, bf16[1,128,2048]{2,1,0:T(8,128)(2,1)}, u32[]{:S(2)}) copy-start(bf16[1,128,2048]{2,1,0:T(8,128)(2,1)} %c_ref.1) | copy-start | bytes 1572868
